TPU v7x, 128 devices: a whole 4x4x4 slice. The times are simulated.
128 devices in a mesh: grp: 2 (over x_hi), row: 8 (over x_lo, z), col: 8 (over y, core).
Axes of the slice: x: 4 (x_hi: 2, x_lo: 2; x = x_hi * 2 + x_lo), y: 4, z: 4, core: 2. Of those that a mesh axis runs over, the one named last changes fastest.
Arguments:
- activations: bfloat16 [256, 64, 8192], P(('grp', 'col'), None, 'row'), may hold values from -6 to 6
- out_grads: bfloat16 [256, 64, 8192], P(('grp', 'col'), None, 'row'), may hold values from -6 to 6
- proj_in: bfloat16 [8192, 128], P('row'), may hold values from -0.0625 to 0.0625
- proj_out: bfloat16 [8192, 128], P('row'), may hold values from -0.0625 to 0.0625
- fisher_inv: float32 [16384, 16384], P('row', ('grp', 'col')), may hold values from -1 to 4, as said below
- store: bfloat16 [32768, 16384], P('row', ('grp', 'col')), may hold values from -0.046875 to 0.046875
- lengths: int32 [256], P(('grp', 'col')), may hold values from 1 to 64, as said below
- judge_ids: int32 [256], replicated, may hold values from 0 to 127, as said below
Outputs:
- node_scores: float32 [32768, 128], P('row')
Inputs may be any that keep to these rules, and one draw needn't show every extreme that they name: lengths[b] is how many of branch b's first token slots count; the rest are padding. `judge_ids`: every node id names at least one branch. fisher_inv is symmetric.
All inputs are finite; a program needn't handle non-finite values.
Results may differ from a plain program's by a relative error of at most 0.0029.
Values may be sent and summed in bfloat16 or wider, within the bound.
A program may use at most 128 MiB of HBM per device.

v0:
```python
import math

import jax
import jax.numpy as jnp
from jax import lax
from jax.sharding import PartitionSpec as P


def local(activations, out_grads, proj_in, proj_out, fisher_inv, store, lengths, judge_ids):
    high = lax.Precision.HIGHEST
    br_here, tok_slots, width_here = activations.shape
    rank = proj_in.shape[1]
    act_proj = jnp.dot(
        activations.reshape(br_here * tok_slots, width_here),
        proj_in,
        preferred_element_type=jnp.float32,
    )
    grad_proj = jnp.dot(
        out_grads.reshape(br_here * tok_slots, width_here),
        proj_out,
        preferred_element_type=jnp.float32,
    )
    act_proj, grad_proj = lax.psum((act_proj, grad_proj), "row")
    token_mask = (jnp.arange(tok_slots)[None, :] < lengths[:, None]).astype(jnp.float32)
    weighted = grad_proj.reshape(br_here, tok_slots, rank) * token_mask[:, :, None]
    grads = jnp.einsum(
        "bto,bti->boi", weighted, act_proj.reshape(br_here, tok_slots, rank), precision=high
    ) * (1.0 / math.sqrt(tok_slots))
    grads = grads.reshape(br_here, rank * rank)
    rows_here, cols_here = fisher_inv.shape
    grad_block = lax.all_to_all(grads, ("grp", "col"), split_axis=1, concat_axis=0, tiled=True)
    partial_value = lax.dot_general(
        fisher_inv, grad_block, (((1,), (1,)), ((), ())), precision=high
    )
    pre_rows = lax.psum(partial_value, ("grp", "col")).astype(jnp.bfloat16)
    pre_all = lax.all_gather(pre_rows, "row", axis=0, tiled=True)
    column = lax.axis_index(("grp", "col"))
    pre_block = lax.dynamic_slice_in_dim(pre_all, column * cols_here, cols_here, 0)
    scores_part = jnp.dot(store, pre_block, preferred_element_type=jnp.float32)
    node_count = judge_ids.shape[0] // 2
    onehot = (judge_ids[:, None] == jnp.arange(node_count)[None, :]).astype(jnp.float32)
    scores = lax.psum(scores_part, ("grp", "col"))
    return jnp.dot(scores, onehot, precision=high)


def solution(mesh):
    placed = (
        P(("grp", "col"), None, "row"),
        P(("grp", "col"), None, "row"),
        P("row", None),
        P("row", None),
        P("row", ("grp", "col")),
        P("row", ("grp", "col")),
        P(("grp", "col")),
        P(),
    )
    return jax.shard_map(
        local, mesh=mesh, in_specs=placed, out_specs=P("row", None), check_vma=False
    )
```

profile of v0, /device:TPU:1, one launch (start us, length us, event | category | flops | bytes accessed | tf_op | source)
XLA Modules:
  0.0 474.9 jit_solution(9242926295125779573)
XLA Ops:
  6.5 0.0 copy-start
  6.5 0.0 copy-start.2
  6.5 0.0 all-reduce.7.cloned.1.call-start
  6.5 1.6 copy-done
  8.1 2.5 fusion.8
  10.6 3.1 fusion.7
  13.7 0.0 all-reduce.7.cloned.1.call-update
  13.7 0.0 all-gather.2.cloned.1.call-start
  13.8 0.0 copy-done.2
  13.8 0.1 fusion.5
  13.8 75.7 %all-reduce.7.cloned.1.call-done = (f32[16,64,128]{2,1,0:T(8,128)}, f32[16,64,128]{2,1,0:T(8,128)}) async-done(((f32[16,64,128]{2,1,0:T(8,128)}, f32[16,64,128]{2,1,0:T(8,128)}), (f32[16,64,128]{2,1,0:T(8,128)}, f32[16,64,128]{2,1,0:T(8,128)})) %all-reduce.7.cloned.1.call-update) | async-done | bytes 1048592 | tf_op jit(solution)/shard_map/psum | solution.py:23
  89.6 3.2 convolution_multiply_fusion
  92.8 1.1 all_to_all.14
  93.9 1.8 copy.9
  95.7 28.9 %all_to_all.19 = f32[16,16,1024]{2,0,1:T(8,128)S(1)} all-to-all(f32[16,16,1024]{2,0,1:T(8,128)S(1)} %copy.9), channel_id=1, replica_groups=mesh['grp'=2,'row'=8,'col'=8] {'grp','col'}, dimensions={1} | all-to-all | bytes 2097152 | tf_op jit(solution)/shard_map/all_to_all | solution.py:31
  124.6 10.6 %convolution_bitcast_fusion.1 = f32[2048,256]{0,1:T(8,128)} fusion(f32[256,1024]{1,0:T(8,128)S(1)} %bitcast.21, f32[2048,1024]{1,0:T(8,128)} %param.12), kind=kOutput, calls=%fused_computation.1 | convolution fusion | flops 6442450944 | bytes 11534336 | tf_op jit(solution)/shard_map/dot_general | solution.py:32
  135.2 74.6 %all-reduce.8 = bf16[2048,256]{0,1:T(8,128)(2,1)} all-reduce(f32[2048,256]{0,1:T(8,128)} %convolution_bitcast_fusion.1), channel_id=1, replica_groups=mesh['grp'=2,'row'=8,'col'=8] {'grp','col'}, use_global_device_ids=true, to_apply=%region_2.0 | all-reduce | flops 524288 | bytes 3145728 | tf_op jit(solution)/shard_map/psum | solution.py:35
  209.7 0.0 all-gather.2.cloned.1.call-update
  209.8 0.2 all-reduce.5.cloned.1.call-start
  210.0 94.9 %all-gather.2.cloned.1.call-done = bf16[16384,256]{0,1:T(8,128)(2,1)} async-done(((bf16[2048,256]{0,1:T(8,128)(2,1)}), bf16[16384,256]{0,1:T(8,128)(2,1)}) %all-gather.2.cloned.1.call-update) | async-done | bytes 8388624 | tf_op jit(solution)/shard_map/all_gather | solution.py:36
  304.9 7.9 %convolution_bitcast_fusion = f32[4096,256]{0,1:T(8,128)} fusion(bf16[4096,1024]{1,0:T(8,128)(2,1)} %param.13, bf16[16384,256]{0,1:T(8,128)(2,1)} %all-gather.2.cloned.1.call-done, s32[]{:T(128)S(6)} %select_n.3), kind=kOutput, calls=%fused_computation | convolution fusion | flops 2147483648 | bytes 13107204 | tf_op jit(solution)/shard_map/dot_general | solution.py:39
  312.8 0.0 copy-start.1
  312.8 0.0 all-reduce.5.cloned.1.call-update
  312.8 148.6 %all-reduce.5.cloned.1.call-done = f32[4096,256]{0,1:T(8,128)} async-done(((f32[4096,256]{0,1:T(8,128)}), f32[4096,256]{0,1:T(8,128)}) %all-reduce.5.cloned.1.call-update) | async-done | bytes 4194320 | tf_op jit(solution)/shard_map/psum | solution.py:42
  461.4 0.0 copy-done.1
  461.4 7.0 %fusion.3 = f32[4096,128]{1,0:T(8,128)} fusion(f32[4096,256]{0,1:T(8,128)} %all-reduce.5.cloned.1.call-done, s32[256]{0:T(256)S(1)} %copy-done.1), kind=kOutput, calls=%fused_computation.7 | convolution fusion | flops 1610645504 | bytes 6292480 | tf_op jit(solution)/shard_map/dot_general | solution.py:43
Async XLA Ops:
  6.5 1.6 copy-start
  6.5 7.2 %copy-start.2 = (s32[16]{0:T(128)S(1)}, s32[16]{0:T(128)}, u32[]{:S(2)}) copy-start(s32[16]{0:T(128)} %param.14) | copy-start | bytes 196
  6.5 83.0 %all-reduce.7.cloned.1.call-start = ((), (), s32[]{:S(2)}) async-start(), calls=%async_computation.3 | async-start | bytes 2097152 | tf_op jit(solution)/shard_map/psum | solution.py:23
  13.7 291.2 %all-gather.2.cloned.1.call-start = ((), (), s32[]{:S(2)}) async-start(), calls=%async_computation.1 | async-start | bytes 9437184 | tf_op jit(solution)/shard_map/all_gather | solution.py:36
  209.8 251.6 %all-reduce.5.cloned.1.call-start = ((), (), s32[]{:S(2)}) async-start(), calls=%async_computation.2 | async-start | bytes 8388608 | tf_op jit(solution)/shard_map/psum | solution.py:42
  312.8 148.6 %copy-start.1 = (s32[256]{0:T(256)S(1)}, s32[256]{0:T(256)}, u32[]{:S(2)}) copy-start(s32[256]{0:T(256)} %param.15) | copy-start | bytes 3076
Sparse Core Ops, SparseCore 0:
  13.8 75.7 all-reduce.6
  209.9 94.9 all-gather.1
  313.0 148.3 all-reduce.4
where the time goes:
time: 475 us
  waiting for transfers between devices  319 us (67%)
  blocking collectives  103 us (22%)
  matrix products  34.2 us (7%)
  between operations  13.1 us (3%)
    psum x1, waiting for transfers between devices, local(): scores = lax.psum(scores_part, ('grp', 'col'))  149 us
    all_gather x1, waiting for transfers between devices, local(): pre_all = lax.all_gather(pre_rows, 'row', axis=0, tiled=True)  94.9 us
    psum x1, waiting for transfers between devices, local(): act_proj, grad_proj = lax.psum((act_proj, grad_proj), 'row')  75.7 us
    psum x1, blocking collectives, local(): pre_rows = lax.psum(partial_value, ('grp', 'col')).astype(jnp.bfloat16)  74.6 us
    all_to_all x1, blocking collectives, local(): lax.all_to_all(grads, ('grp', 'col'), split_axis=1, concat_axis=0, tiled=...  28.9 us
    dot_general x1, matrix products, local(): lax.dot_general(fisher_inv, grad_block, (((1,), (1,)), ((), ())), precisi...  10.6 us
  transfers between devices with their start and end apart: 3, of which 3 were waited for; matrix products, arithmetic and copies ran while one was open for 0% of the time, Pallas kernels for 0%

commit v1 on v0

v1 whole, which is shorter than its diff:
```python
import functools
import math

import jax
import jax.numpy as jnp
from jax import lax
from jax.experimental import pallas as pl
from jax.experimental.pallas import tpu as pltpu
from jax.sharding import PartitionSpec as P

MESH = pl.DeviceIdType.MESH
F32 = jnp.float32
BF16 = jnp.bfloat16
SPAN = 80.0
MROWS = 16


def bound(x):
    top = jnp.max(jnp.abs(x), axis=0, keepdims=True)
    return (top * 1.01 + 1e-36).astype(BF16)


def encode(x, m):
    y = jnp.exp(jnp.abs(x) * (SPAN / m) - 0.5 * SPAN)
    return jnp.where(x < 0, -y, y).astype(BF16)


def decode(y, m):
    y = y.astype(F32)
    t = (jnp.log(jnp.abs(y)) + 0.5 * SPAN) * (m / SPAN)
    return jnp.where(y < 0, -t, t)


def pack(ref, start, x, mstart, mrows=MROWS):
    m = bound(x)
    rows = x.shape[0]
    ref[start:start + rows, :] = encode(x, m.astype(F32))
    ref[mstart:mstart + mrows, :] = jnp.broadcast_to(m, (mrows, x.shape[1]))


def unpack(ref, start, rows, mstart):
    return decode(ref[start:start + rows, :], ref[mstart:mstart + 16, :][:1].astype(F32))


def split(x):
    hi = x.astype(BF16)
    return hi, (x - hi.astype(F32)).astype(BF16)


def dot(a, b):
    return jnp.dot(a, b, preferred_element_type=F32)


def kernel(
    act, og, pin, pout, fish, store, lens, ids, out,
    actv, ogv, pinv, poutv, fv, fhi, flo, sv,
    p1s, p1r, acc_a, acc_g, p2s, p2r, p3, gf, amat,
    p4s, p4r, acc4, p5, p6s, p6r, p7s, p7r, acc7, ob,
    ld1, ldw, ldf, lds, ldo,
    p1ss, p1rs, p2ss, p2rs, p3ss, p3rs, f3ss, f3rs, p4ss, p4rs, p5ss, p5rs,
    p6ss, p6rs, p7ss, p7rs, p8ss, p8rs, f8ss, f8rs,
):
    g = lax.axis_index("grp")
    r = lax.axis_index("row")
    col = lax.axis_index("col")
    y, core = col // 2, col % 2
    q = g * 4 + y
    c = q * 2 + core
    sib = col + 1 - 2 * core

    def ahead(i, k):
        return ((i // 4 + k // 4) % 2) * 4 + (i % 4 + k % 4) % 4

    def behind(i, k):
        return ((i // 4 + k // 4) % 2) * 4 + (i % 4 + 4 - k % 4) % 4

    def to_row(i):
        return {"row": i}

    def to_chip(i):
        return {"grp": i // 4, "col": (i % 4) * 2 + core}

    to_sib = {"col": sib}

    def remote(src, dst, ss, rs, dev):
        return pltpu.make_async_remote_copy(
            src_ref=src, dst_ref=dst, send_sem=ss, recv_sem=rs, device_id=dev, device_id_type=MESH)

    pltpu.make_async_copy(pin, pinv, ldw.at[0]).start()
    pltpu.make_async_copy(pout, poutv, ldw.at[1]).start()

    def tokens(k):
        rows = pl.ds(pl.multiple_of(ahead(r, k % 8) * 128, 128), 128)
        return (pltpu.make_async_copy(act.at[rows, :], actv.at[rows, :], ld1.at[0, k]),
                pltpu.make_async_copy(og.at[rows, :], ogv.at[rows, :], ld1.at[1, k]))

    def start_tokens(k, _):
        for cp in tokens(k):
            cp.start()
        return 0
    lax.fori_loop(1, 9, start_tokens, 0)

    barrier = pltpu.get_barrier_semaphore()

    def greet(k, _):
        pl.semaphore_signal(barrier, inc=1, device_id=to_row(ahead(r, k)), device_id_type=MESH)
        pl.semaphore_signal(barrier, inc=1, device_id=to_chip(ahead(q, k)), device_id_type=MESH)
        return 0
    lax.fori_loop(1, 8, greet, 0)
    pl.semaphore_signal(barrier, inc=1, device_id=to_sib, device_id_type=MESH)
    pl.semaphore_wait(barrier, 15)

    def project(k):
        rows = pl.ds(pl.multiple_of(ahead(r, k % 8) * 128, 128), 128)
        for cp in tokens(k):
            cp.wait()
        return dot(actv[rows, :], pinv[...]), dot(ogv[rows, :], poutv[...])

    pltpu.make_async_copy(pin, pinv, ldw.at[0]).wait()
    pltpu.make_async_copy(pout, poutv, ldw.at[1]).wait()

    def p1_copy(k):
        return remote(p1s.at[k], p1r.at[k], p1ss.at[k], p1rs.at[k], to_row(ahead(r, k)))

    def p1_send(k, _):
        a, b = project(k)
        buf = p1s.at[k]
        pack(buf, 0, a, 256)
        pack(buf, 128, b, 272)
        p1_copy(k).start()
        return 0
    lax.fori_loop(1, 8, p1_send, 0)
    a, b = project(8)
    acc_a[...] = a
    acc_g[...] = b

    def f_load(i):
        rows = pl.ds(pl.multiple_of(i * 256, 256), 256)
        return pltpu.make_async_copy(fish.at[rows, :], fv.at[rows, :], ldf.at[i])

    def f_start(i, _):
        f_load(i).start()
        return 0
    lax.fori_loop(0, 8, f_start, 0)

    def f_split(i, _):
        f_load(i).wait()

        def part(j, _):
            rows = pl.ds(pl.multiple_of(i * 256 + j * 32, 32), 32)
            hi, lo = split(fv[rows, :])
            fhi[rows, :] = hi
            flo[rows, :] = lo
            return 0
        lax.fori_loop(0, 8, part, 0)
        return 0
    lax.fori_loop(0, 8, f_split, 0)
    store_copy = pltpu.make_async_copy(store, sv, lds)
    store_copy.start()

    def p1_recv(k, _):
        p1_copy(k).wait_recv()
        buf = p1r.at[k]
        acc_a[...] += unpack(buf, 0, 128, 256)
        acc_g[...] += unpack(buf, 128, 128, 272)
        return 0
    lax.fori_loop(1, 8, p1_recv, 0)

    place = lax.broadcasted_iota(jnp.int32, (128, 128), 0)
    limit = jnp.where(place < 64, lens[2 * r], lens[2 * r + 1] + 64)
    weighted = jnp.where(place < limit, acc_g[...], 0.0)
    for j in range(2):
        p2s[j] = lax.dot_general(
            weighted[64 * j:64 * j + 64], acc_a[64 * j:64 * j + 64, :], (((0,), (0,)), ((), ())),
            precision=lax.Precision.HIGHEST, preferred_element_type=F32) * 0.125

    def p2_copy(k):
        dest = ahead(r, k)
        return remote(p2s.at[:, pl.ds(pl.multiple_of(dest * 16, 16), 16), :], p2r.at[r],
                      p2ss.at[k], p2rs.at[k], to_row(dest))

    def p2_wait(k):
        return remote(p2s.at[:, pl.ds(0, 16), :], p2r.at[behind(r, k)], p2ss.at[k], p2rs.at[k],
                      to_row(ahead(r, k)))

    def p2_send(k, _):
        p2_copy(k).start()
        return 0
    lax.fori_loop(1, 8, p2_send, 0)
    p2r[r] = p2s[:, pl.ds(pl.multiple_of(r * 16, 16), 16), :]

    def p2_recv(k, _):
        p2_wait(k).wait_recv()
        return 0
    lax.fori_loop(1, 8, p2_recv, 0)

    pack(p3.at[c], 0, p2r[...].reshape(256, 128), 256)

    def gather(buf, slot_of, ss, rs, fss, frs, use):
        mine = slot_of(q, core)

        def first(k):
            return remote(buf.at[mine], buf.at[mine], ss.at[k], rs.at[k], to_chip(ahead(q, k)))

        def arrives(k):
            slot = slot_of(behind(q, k), core)
            return remote(buf.at[slot], buf.at[slot], ss.at[k], rs.at[k], to_chip(ahead(q, k)))

        def onward(k, which):
            slot = slot_of(behind(q, k), which)
            return remote(buf.at[slot], buf.at[slot], fss.at[k], frs.at[k], to_sib)

        def go(k, _):
            first(k).start()
            return 0
        lax.fori_loop(1, 8, go, 0)
        onward(0, core).start()
        use(mine)

        def near(k, _):
            arrives(k).wait_recv()
            onward(k, core).start()
            use(slot_of(behind(q, k), core))
            return 0
        lax.fori_loop(1, 8, near, 0)

        def far(k, _):
            onward(k, 1 - core).wait_recv()
            use(slot_of(behind(q, k), 1 - core))
            return 0
        lax.fori_loop(0, 8, far, 0)

        def finish():
            def done(k, _):
                first(k).wait_send()
                return 0
            lax.fori_loop(1, 8, done, 0)

            def done_on(k, _):
                onward(k, core).wait_send()
                return 0
            lax.fori_loop(0, 8, done_on, 0)
        return finish

    def use3(slot):
        gf[pl.ds(pl.multiple_of(slot * 256, 256), 256), :] = unpack(p3.at[slot], 0, 256, 256)

    finish3 = gather(p3, lambda chip, k: chip * 2 + k, p3ss, p3rs, f3ss, f3rs, use3)

    onehot = (lax.broadcasted_iota(jnp.int32, (128, 256), 0) == ids[...]).astype(F32).astype(BF16)

    def fold(o, _):
        hi, lo = split(gf[pl.ds(o, 256, stride=16), :])
        hi, lo = split(dot(onehot, hi) + dot(onehot, lo))
        lanes = pl.ds(pl.multiple_of(o * 128, 128), 128)
        amat[0:128, lanes] = hi
        amat[128:256, lanes] = lo
        return 0
    lax.fori_loop(0, 16, fold, 0)

    def p4_copy(dest):
        return remote(p4s.at[dest], p4r.at[r], p4ss.at[dest], p4rs.at[r], to_row(dest))

    def p4_wait(src):
        return remote(p4s.at[src], p4r.at[src], p4ss.at[src], p4rs.at[src], to_row(src))

    def precondition(k, _):
        p = (r // 2 + k) % 4
        lanes = pl.ds(pl.multiple_of(p * 256, 256), 256)
        both = dot(amat[...], fhi[:, lanes])
        full = both[0:128] + both[128:256] + dot(amat[0:128, :], flo[:, lanes])
        for e in range(2):
            dest = 2 * p + e
            part = full[:, e * 128:(e + 1) * 128]
            pack(p4s.at[dest], 0, part, 128)

            @pl.when(dest != r)
            def _():
                p4_copy(dest).start()

            @pl.when(dest == r)
            def _():
                acc4[...] = part
        return 0
    lax.fori_loop(1, 5, precondition, 0)

    def p4_recv(k, _):
        src = behind(r, k)
        p4_wait(src).wait_recv()
        acc4[...] += unpack(p4r.at[src], 0, 128, 128)
        return 0
    lax.fori_loop(1, 8, p4_recv, 0)

    mine5 = pl.ds(pl.multiple_of(r * 128, 128), 128)
    p5[mine5, :] = acc4[...].T.astype(BF16)

    def p5_copy(k):
        return remote(p5.at[mine5, :], p5.at[mine5, :], p5ss.at[k], p5rs.at[k], to_row(ahead(r, k)))

    def p5_wait(k):
        rows = pl.ds(pl.multiple_of(behind(r, k) * 128, 128), 128)
        return remote(p5.at[rows, :], p5.at[rows, :], p5ss.at[k], p5rs.at[k], to_row(ahead(r, k)))

    def p5_send(k, _):
        p5_copy(k).start()
        return 0
    lax.fori_loop(1, 8, p5_send, 0)
    store_copy.wait()

    def p5_recv(k, _):
        p5_wait(k).wait_recv()
        return 0
    lax.fori_loop(1, 8, p5_recv, 0)

    def score(half, chip):
        rows = pl.ds(pl.multiple_of(half * 2048 + chip * 256, 256), 256)
        return dot(sv[rows, :], p5[...])

    def p6_copy(k):
        return remote(p6s.at[k], p6r.at[k], p6ss.at[k], p6rs.at[k], to_sib)

    def p6_send(i, _):
        k = i % 8
        pack(p6s.at[k], 0, score(1 - core, ahead(q, k)), 256)
        p6_copy(k).start()
        return 0
    lax.fori_loop(1, 9, p6_send, 0)

    def p7_copy(k):
        return remote(p7s.at[k], p7r.at[k], p7ss.at[k], p7rs.at[k], to_chip(ahead(q, k)))

    def chip_sum(k):
        x = score(core, ahead(q, k))
        p6_copy(k).wait_recv()
        return x + unpack(p6r.at[k], 0, 256, 256)

    def p7_send(k, _):
        pack(p7s.at[k], 0, chip_sum(k), 256)
        p7_copy(k).start()
        return 0
    lax.fori_loop(1, 8, p7_send, 0)
    acc7[...] = chip_sum(0)

    def p7_recv(k, _):
        p7_copy(k).wait_recv()
        acc7[...] += unpack(p7r.at[k], 0, 256, 256)
        return 0
    lax.fori_loop(1, 8, p7_recv, 0)

    pack(ob.at[core * 8 + q], 0, acc7[...], 256)

    def leave(slot):
        return pltpu.make_async_copy(ob.at[slot], out.at[slot], ldo.at[slot])

    finish8 = gather(ob, lambda chip, k: k * 8 + chip, p8ss, p8rs, f8ss, f8rs, lambda slot: leave(slot).start())

    def done(k, _):
        p1_copy(k).wait_send()
        p2_wait(k).wait_send()
        p4_wait(ahead(r, k)).wait_send()
        p5_copy(k).wait_send()
        p7_copy(k).wait_send()
        return 0
    lax.fori_loop(1, 8, done, 0)

    def done6(k, _):
        p6_copy(k).wait_send()
        return 0
    lax.fori_loop(0, 8, done6, 0)
    finish3()
    finish8()

    def done_out(k, _):
        leave(k).wait()
        return 0
    lax.fori_loop(0, 16, done_out, 0)


def local(activations, out_grads, proj_in, proj_out, fisher_inv, store, lengths, judge_ids):
    br_here, toks, width = activations.shape
    any_spec = pl.BlockSpec(memory_space=pl.ANY)
    dma = pltpu.SemaphoreType.DMA
    coded = pl.pallas_call(
        kernel,
        out_shape=jax.ShapeDtypeStruct((16, 272, 128), BF16),
        in_specs=[any_spec] * 6 + [pl.BlockSpec(memory_space=pltpu.SMEM), pl.BlockSpec(memory_space=pltpu.VMEM)],
        out_specs=any_spec,
        scratch_shapes=[
            pltpu.VMEM((1024, 1024), BF16), pltpu.VMEM((1024, 1024), BF16),
            pltpu.VMEM((1024, 128), BF16), pltpu.VMEM((1024, 128), BF16),
            pltpu.VMEM((2048, 1024), F32), pltpu.VMEM((2048, 1024), BF16), pltpu.VMEM((2048, 1024), BF16),
            pltpu.VMEM((4096, 1024), BF16),
            pltpu.VMEM((8, 288, 128), BF16), pltpu.VMEM((8, 288, 128), BF16),
            pltpu.VMEM((128, 128), F32), pltpu.VMEM((128, 128), F32),
            pltpu.VMEM((2, 128, 128), F32), pltpu.VMEM((8, 2, 16, 128), F32),
            pltpu.VMEM((16, 272, 128), BF16), pltpu.VMEM((4096, 128), F32), pltpu.VMEM((256, 2048), BF16),
            pltpu.VMEM((8, 144, 128), BF16), pltpu.VMEM((8, 144, 128), BF16), pltpu.VMEM((128, 128), F32),
            pltpu.VMEM((1024, 128), BF16),
            pltpu.VMEM((8, 272, 128), BF16), pltpu.VMEM((8, 272, 128), BF16),
            pltpu.VMEM((8, 272, 128), BF16), pltpu.VMEM((8, 272, 128), BF16),
            pltpu.VMEM((256, 128), F32), pltpu.VMEM((16, 272, 128), BF16),
            dma((2, 9)), dma((2,)), dma((8,)), dma(()), dma((16,)),
        ] + [dma((8,)) for _ in range(20)],
        compiler_params=pltpu.CompilerParams(
            collective_id=0, has_side_effects=True, vmem_limit_bytes=56 * 1024 * 1024),
    )(activations.reshape(br_here * toks, width), out_grads.reshape(br_here * toks, width),
      proj_in, proj_out, fisher_inv, store, lengths, judge_ids.reshape(1, -1))
    return decode(coded[:, :256, :], coded[:, 256:257, :].astype(F32)).reshape(4096, 128)


def solution(mesh):
    placed = (
        P(("grp", "col"), None, "row"),
        P(("grp", "col"), None, "row"),
        P("row", None),
        P("row", None),
        P("row", ("grp", "col")),
        P("row", ("grp", "col")),
        P(("grp", "col")),
        P(),
    )
    return jax.shard_map(
        local, mesh=mesh, in_specs=placed, out_specs=P("row", None), check_vma=False
    )
```

time: 475 us -> 79 us (0.17)
  waiting for transfers between devices: 319 us -> 0 us
  blocking collectives: 103 us -> 0 us
  Pallas kernels: 0 us -> 74.8 us
  matrix products: 34.2 us -> 0 us
  between operations: 13.1 us -> 0.01 us
    psum x2 -> x0, waiting for transfers between devices: 224 us -> none  [the longest x1 149 us: local(): scores = lax.psum(scores_part, ('grp', 'col'))]
    all_gather x1 -> x0, waiting for transfers between devices: 94.9 us -> none  [local(): pre_all = lax.all_gather(pre_rows, 'row', axis=0, tiled=True)]
    pallas_call x0 -> x1, Pallas kernels: none -> 74.8 us  [local(): pl.pallas_call(kernel, out_shape=jax.ShapeDtypeStruct((16, 272, 128), BF1...]
    psum x1 -> x0, blocking collectives: 74.6 us -> none  [local(): pre_rows = lax.psum(partial_value, ('grp', 'col')).astype(jnp.bfloat16)]
    dot_general x6 -> x0, matrix products: 34.2 us -> none  [the longest x1 10.6 us: local(): lax.dot_general(fisher_inv, grad_block, (((1,), (1,)), ((), ())), precisi...]
    all_to_all x1 -> x0, blocking collectives: 28.9 us -> none  [local(): lax.all_to_all(grads, ('grp', 'col'), split_axis=1, concat_axis=0, tiled=...]
  transfers between devices with their start and end apart: 3 -> 0, of which waited for: 3 -> 0; matrix products, arithmetic and copies ran while one was open for 0% -> 0% of each run, Pallas kernels for 0% -> 0%
where the time goes in v1:
time: 79 us; the launch traced here: 78.7 us
  Pallas kernels  74.8 us (95%)
  other arithmetic  3.93 us (5%)
    pallas_call x1, Pallas kernels, local(): pl.pallas_call(kernel, out_shape=jax.ShapeDtypeStruct((16, 272, 128), BF1...  74.8 us
    select_n x1, other arithmetic, decode(): return jnp.where(y < 0, -t, t)  3.16 us

profile of v1, /device:TPU:1, one launch (start us, length us, event | category | flops | bytes accessed | tf_op | source)
XLA Modules:
  0.0 78.7 jit_solution(1054824813057721258)
XLA Ops:
  0.0 74.8 %shard_map.82 = bf16[16,272,128]{2,1,0:T(8,128)(2,1)} custom-call(bf16[1024,1024]{1,0:T(8,128)(2,1)} %bitcast.5, bf16[1024,1024]{1,0:T(8,128)(2,1)} %bitcast.6, bf16[1024,128]{1,0:T(8,128)(2,1)} %pin.1, bf16[1024,128]{1,0:T(8,128)(2,1)} %pout.1, f32[2048,1024]{1,0:T(8,128)} %fish.1, bf16[4096,1024]{1,0:T(8,128)(2,1)} %store.1, s32[16]{0:T(128)} %lens.1, ...), custom_call_target="tpu_custom_call" | custom-call | tf_op jit(solution)/shard_map/pallas_call | solution.py:383
  74.8 0.8 convert_multiply_fusion
  75.6 3.2 %negate_select_fusion = f32[16,256,128]{2,1,0:T(8,128)} fusion(f32[16,128]{1,0:T(8,128)S(1)} %bitcast.7, bf16[16,272,128]{2,1,0:T(8,128)(2,1)} %shard_map.82), kind=kLoop, calls=%fused_computation | loop fusion | flops 3670016 | bytes 3153920 | tf_op jit(solution)/shard_map/jit(_where)/select_n | solution.py:31

commit v2 on v0

v2 whole, which is shorter than its diff:
```python
import jax
import jax.numpy as jnp
from jax import lax
from jax.experimental import pallas as pl
from jax.experimental.pallas import tpu as pltpu
from jax.sharding import PartitionSpec as P

MESH = pl.DeviceIdType.MESH
F32 = jnp.float32
BF16 = jnp.bfloat16
SPAN = 80.0


def bound(x):
    top = jnp.max(jnp.abs(x), axis=0, keepdims=True)
    return (top * 1.01 + 1e-36).astype(BF16)


def encode(x, m):
    y = jnp.exp(jnp.abs(x) * (SPAN / m) - 0.5 * SPAN)
    return jnp.where(x < 0, -y, y).astype(BF16)


def decode(y, m):
    y = y.astype(F32)
    t = (jnp.log(jnp.abs(y)) + 0.5 * SPAN) * (m / SPAN)
    return jnp.where(y < 0, -t, t)


def pack(ref, x):
    rows = x.shape[0]
    m = bound(x)
    ref[0:rows, :] = encode(x, m.astype(F32))
    ref[rows:rows + 16, :] = jnp.broadcast_to(m, (16, x.shape[1]))


def unpack(ref):
    rows = ref.shape[0] - 16
    return decode(ref[0:rows, :], ref[rows:rows + 16, :][:1].astype(F32))


def split(x):
    hi = x.astype(BF16)
    return hi, (x - hi.astype(F32)).astype(BF16)


def dot(a, b):
    return jnp.dot(a, b, preferred_element_type=F32)


def loop(lo, hi, body):
    def step(i, _):
        body(i)
        return 0
    lax.fori_loop(lo, hi, step, 0)


def kernel(
    act, og, pin, pout, fish, store, lens, ids, out,
    actv, ogv, pinv, poutv, fv, fhi, flo, sv,
    proj, p1s, p1r, acc1, p2s, p2r, p3, gf, amat,
    p4s, p4r, acc4, p5, pre, p6s, p6r, p7s, p7r, acc7, ob,
    ldw, ld1, ldf, lds, ldo,
    p1ss, p1rs, p2ss, p2rs, p3ss, p3rs, f3ss, f3rs, p4ss, p4rs, p5ss, p5rs,
    p6ss, p6rs, p7ss, p7rs, p8ss, p8rs, f8ss, f8rs,
):
    g = lax.axis_index("grp")
    r = lax.axis_index("row")
    col = lax.axis_index("col")
    y, core = lax.div(col, 2), lax.rem(col, 2)
    q = g * 4 + y
    sib = col + 1 - 2 * core
    rx, rz = lax.div(r, 4), lax.rem(r, 4)
    peers = range(1, 8)
    both = range(2)

    def around(hi, lo, k, sign):
        return lax.rem(hi + k // 4, 2) * 4 + lax.rem(lo + (k % 4 if sign > 0 else 4 - k % 4), 4)

    row_to = [around(rx, rz, k, 1) for k in range(8)]
    row_from = [around(rx, rz, k, -1) for k in range(8)]
    chip_to = [around(g, y, k, 1) for k in range(8)]
    chip_from = [around(g, y, k, -1) for k in range(8)]
    to_row = [{"row": i} for i in row_to]
    to_chip = [{"grp": lax.rem(g + k // 4, 2), "col": lax.rem(y + k % 4, 4) * 2 + core} for k in range(8)]
    to_sib = {"col": sib}

    def remote(src, dst, ss, rs, dev):
        return pltpu.make_async_remote_copy(
            src_ref=src, dst_ref=dst, send_sem=ss, recv_sem=rs, device_id=dev, device_id_type=MESH)

    load_w = [pltpu.make_async_copy(pin, pinv, ldw.at[0]), pltpu.make_async_copy(pout, poutv, ldw.at[1])]

    def load_tokens(h, which):
        rows = pl.ds(512 * h, 512)
        src, dst = ((act, actv), (og, ogv))[which]
        return pltpu.make_async_copy(src.at[rows, :], dst.at[rows, :], ld1.at[h, which])

    load_w[0].start()
    load_tokens(0, 0).start()
    load_w[1].start()
    load_tokens(0, 1).start()
    load_tokens(1, 0).start()
    load_tokens(1, 1).start()
    barrier = pltpu.get_barrier_semaphore()
    for k in peers:
        pl.semaphore_signal(barrier, inc=1, device_id=to_row[k], device_id_type=MESH)
        pl.semaphore_signal(barrier, inc=1, device_id=to_chip[k], device_id_type=MESH)
    pl.semaphore_signal(barrier, inc=1, device_id=to_sib, device_id_type=MESH)

    def f_load(i):
        rows = pl.ds(pl.multiple_of(i * 256, 256), 256)
        return pltpu.make_async_copy(fish.at[rows, :], fv.at[rows, :], ldf.at[i])

    def f_split(i):
        f_load(i).wait()

        def part(j):
            rows = pl.ds(pl.multiple_of(i * 256 + j * 32, 32), 32)
            hi, lo = split(fv[rows, :])
            fhi[rows, :] = hi
            flo[rows, :] = lo
        loop(0, 8, part)

    def p1_copy(h, k):
        return remote(p1s.at[h, k], p1r.at[h, k], p1ss.at[h, k], p1rs.at[h, k], to_row[k])

    for h in both:
        rows = slice(512 * h, 512 * h + 512)
        if h == 0:
            load_w[0].wait()
        load_tokens(h, 0).wait()
        proj[:, 0:128] = dot(actv[rows, :], pinv[...])
        if h == 0:
            load_w[1].wait()
        load_tokens(h, 1).wait()
        proj[:, 128:256] = dot(ogv[rows, :], poutv[...])
        for k in peers:
            pack(p1s.at[h, k], proj[pl.ds(pl.multiple_of(row_to[k] * 64, 64), 64), :])
            if h == 0 and k == 1:
                pl.semaphore_wait(barrier, 15)
            p1_copy(h, k).start()
        acc1[h] = proj[pl.ds(pl.multiple_of(r * 64, 64), 64), :]

    loop(0, 8, lambda i: f_load(i).start())
    onehot = (lax.broadcasted_iota(jnp.int32, (128, 256), 0) == ids[...]).astype(F32).astype(BF16)
    place = (lax.broadcasted_iota(jnp.int32, (256, 256), 0), lax.broadcasted_iota(jnp.int32, (256, 256), 1))
    moved = lax.rem(lax.div(place[1], 8), 16) * 16 + lax.div(place[1], 128) * 8 + lax.rem(place[1], 8)
    onehot = dot(onehot, (place[0] == moved).astype(F32).astype(BF16)).astype(BF16)
    loop(0, 5, f_split)

    def p2_copy(h, k):
        rows = pl.ds(pl.multiple_of(row_to[k] * 16, 16), 16)
        return remote(p2s.at[h, rows, :], p2r.at[h, pl.ds(pl.multiple_of(r * 16, 16), 16), :],
                      p2ss.at[h, k], p2rs.at[h, k], to_row[k])

    def p2_arrive(h, k):
        rows = pl.ds(pl.multiple_of(row_from[k] * 16, 16), 16)
        return remote(p2s.at[h, rows, :], p2r.at[h, rows, :], p2ss.at[h, k], p2rs.at[h, k], to_row[k])

    for h in both:
        for k in peers:
            p1_copy(h, k).wait_recv()
            acc1[h] += unpack(p1r.at[h, k])
        total = acc1[h]
        live = lax.broadcasted_iota(jnp.int32, (64, 128), 0) < lens[8 * h + r]
        ahi, alo = split(total[:, 0:128])
        ghi, glo = split(jnp.where(live, total[:, 128:256], 0.0) * 0.125)
        p2s[h] = lax.dot_general(
            jnp.concatenate([ghi, ghi, glo], axis=0), jnp.concatenate([ahi, alo, ahi], axis=0),
            (((0,), (0,)), ((), ())), preferred_element_type=F32)
        for k in peers:
            p2_copy(h, k).start()
        own = pl.ds(pl.multiple_of(r * 16, 16), 16)
        p2r[h, own, :] = p2s[h, own, :]
    store_copy = pltpu.make_async_copy(store, sv, lds)
    store_copy.start()
    loop(5, 8, f_split)

    def slot3(chip, k):
        return chip * 2 + k

    mine3 = slot3(q, core)

    def p3_copy(h, k):
        return remote(p3.at[h, mine3], p3.at[h, mine3], p3ss.at[h, k], p3rs.at[h, k], to_chip[k])

    def p3_arrive(h, k):
        slot = slot3(chip_from[k], core)
        return remote(p3.at[h, slot], p3.at[h, slot], p3ss.at[h, k], p3rs.at[h, k], to_chip[k])

    def p3_onward(h, k, which):
        slot = slot3(chip_from[k], which)
        return remote(p3.at[h, slot], p3.at[h, slot], f3ss.at[h, k], f3rs.at[h, k], to_sib)

    def use3(h, slot):
        x = unpack(p3.at[h, slot])
        rows = pl.ds(pl.multiple_of(h * 128 + slot * 8, 8), 8)
        for o in range(16):
            gf[o // 2, rows, (o % 2) * 128:(o % 2) * 128 + 128] = x[8 * o:8 * o + 8]

    for h in both:
        for k in peers:
            p2_arrive(h, k).wait_recv()
        pack(p3.at[h, mine3], jnp.concatenate([p2r[h, pl.ds(o, 8, stride=16), :] for o in range(16)], axis=0))
        for k in peers:
            p3_copy(h, k).start()
        p3_onward(h, 0, core).start()
        use3(h, mine3)
    for h in both:
        for k in peers:
            p3_arrive(h, k).wait_recv()
            p3_onward(h, k, core).start()
            use3(h, slot3(chip_from[k], core))
        for k in range(8):
            p3_onward(h, k, 1 - core).wait_recv()
            use3(h, slot3(chip_from[k], 1 - core))

    for j in range(8):
        hi, lo = split(gf[j])
        hi, lo = split(dot(onehot, hi) + dot(onehot, lo))
        amat[0:128, 256 * j:256 * j + 256] = hi
        amat[128:256, 256 * j:256 * j + 256] = lo

    def p4_copy(dest):
        return remote(p4s.at[dest], p4r.at[r], p4ss.at[dest], p4rs.at[r], {"row": dest})

    def p4_arrive(k):
        src = row_from[k]
        return remote(p4s.at[src], p4r.at[src], p4ss.at[src], p4rs.at[src], to_row[k])

    def precondition(k):
        p = lax.rem(lax.div(r, 2) + k, 4)
        lanes = pl.ds(pl.multiple_of(p * 256, 256), 256)
        two = dot(amat[...], fhi[:, lanes])
        full = two[0:128] + two[128:256] + dot(amat[0:128, :], flo[:, lanes])
        for e in both:
            dest = 2 * p + e
            part = full[:, e * 128:(e + 1) * 128]
            pack(p4s.at[dest], part)

            @pl.when(dest != r)
            def _():
                p4_copy(dest).start()

            @pl.when(dest == r)
            def _():
                acc4[...] = part
    loop(1, 5, precondition)

    for k in peers:
        p4_arrive(k).wait_recv()
        acc4[...] += unpack(p4r.at[row_from[k]])

    def p5_copy(k):
        return remote(p5.at[r], p5.at[r], p5ss.at[k], p5rs.at[k], to_row[k])

    def p5_arrive(k):
        return remote(p5.at[row_from[k]], p5.at[row_from[k]], p5ss.at[k], p5rs.at[k], to_row[k])

    def use5(i, x):
        hi, lo = split(x)
        rows = pl.ds(pl.multiple_of(i * 128, 128), 128)
        pre[rows, 0:128] = hi
        pre[rows, 128:256] = lo

    own5 = acc4[...].T
    pack(p5.at[r], own5)
    for k in peers:
        p5_copy(k).start()
    use5(r, own5)
    store_copy.wait()
    for k in peers:
        for h in both:
            p1_copy(h, k).wait_send()
            p2_copy(h, k).wait_send()
    for k in peers:
        p5_arrive(k).wait_recv()
        use5(row_from[k], unpack(p5.at[row_from[k]]))

    def score(half, pair):
        rows = pl.ds(pl.multiple_of(half * 2048 + pair * 512, 512), 512)
        two = dot(sv[rows, :], pre[...])
        return two[:, 0:128] + two[:, 128:256]

    def p6_copy(t):
        return remote(p6s.at[t], p6r.at[t], p6ss.at[t], p6rs.at[t], to_sib)

    def p6_send(k):
        t = lax.rem(lax.div(q, 2) + k, 4)
        p6s[t] = score(1 - core, t)
        p6_copy(t).start()
    loop(1, 5, p6_send)

    def p7_copy(dest):
        return remote(p7s.at[dest], p7r.at[q], p7ss.at[dest], p7rs.at[q],
                      {"grp": lax.div(dest, 4), "col": lax.rem(dest, 4) * 2 + core})

    def p7_arrive(k):
        src = chip_from[k]
        return remote(p7s.at[src], p7r.at[src], p7ss.at[src], p7rs.at[src], to_chip[k])

    def p7_send(k):
        t = lax.rem(lax.div(q, 2) + k, 4)
        x = score(core, t)
        p6_copy(t).wait_recv()
        x = x + p6r[t]
        for e in both:
            dest = 2 * t + e
            part = x[256 * e:256 * e + 256]
            pack(p7s.at[dest], part)

            @pl.when(dest != q)
            def _():
                p7_copy(dest).start()

            @pl.when(dest == q)
            def _():
                acc7[...] = part
    loop(1, 5, p7_send)

    for k in peers:
        p4_copy(row_to[k]).wait_send()
        p5_copy(k).wait_send()
        for h in both:
            p3_copy(h, k).wait_send()
    for k in range(8):
        for h in both:
            p3_onward(h, k, core).wait_send()

    for k in peers:
        p7_arrive(k).wait_recv()
        acc7[...] += unpack(p7r.at[chip_from[k]])

    def place8(chip, which):
        return pl.ds(pl.multiple_of(which * 2048 + chip * 256, 256), 256)

    mine8 = place8(q, core)
    ob[mine8, :] = acc7[...].astype(BF16)

    def p8_copy(k):
        return remote(ob.at[mine8, :], ob.at[mine8, :], p8ss.at[k], p8rs.at[k], to_chip[k])

    def p8_arrive(k):
        rows = place8(chip_from[k], core)
        return remote(ob.at[rows, :], ob.at[rows, :], p8ss.at[k], p8rs.at[k], to_chip[k])

    def p8_onward(k, which):
        rows = place8(chip_from[k], which)
        return remote(ob.at[rows, :], ob.at[rows, :], f8ss.at[k], f8rs.at[k], to_sib)

    def leave(k, which):
        rows = place8(chip_from[k], which)
        return pltpu.make_async_copy(ob.at[rows, :], out.at[rows, :], ldo.at[k, which])

    for k in peers:
        p8_copy(k).start()
    p8_onward(0, core).start()
    leave(0, core).start()
    for k in peers:
        p7_copy(chip_to[k]).wait_send()
    loop(0, 4, lambda t: p6_copy(t).wait_send())
    for k in peers:
        p8_arrive(k).wait_recv()
        p8_onward(k, core).start()
        leave(k, core).start()
    for k in range(8):
        p8_onward(k, 1 - core).wait_recv()
        leave(k, 1 - core).start()
    for k in peers:
        p8_copy(k).wait_send()
    for k in range(8):
        p8_onward(k, core).wait_send()
        leave(k, core).wait()
        leave(k, 1 - core).wait()


def local(activations, out_grads, proj_in, proj_out, fisher_inv, store, lengths, judge_ids):
    br_here, toks, width = activations.shape
    any_spec = pl.BlockSpec(memory_space=pl.ANY)
    dma = pltpu.SemaphoreType.DMA
    vmem = pltpu.VMEM
    sums = pl.pallas_call(
        kernel,
        out_shape=jax.ShapeDtypeStruct((4096, 128), BF16),
        in_specs=[any_spec] * 6 + [pl.BlockSpec(memory_space=pltpu.SMEM), pl.BlockSpec(memory_space=pltpu.VMEM)],
        out_specs=any_spec,
        scratch_shapes=[
            vmem((1024, 1024), BF16), vmem((1024, 1024), BF16), vmem((1024, 128), BF16), vmem((1024, 128), BF16),
            vmem((2048, 1024), F32), vmem((2048, 1024), BF16), vmem((2048, 1024), BF16), vmem((4096, 1024), BF16),
            vmem((512, 256), F32), vmem((2, 8, 80, 256), BF16), vmem((2, 8, 80, 256), BF16), vmem((2, 64, 256), F32),
            vmem((2, 128, 128), F32), vmem((2, 128, 128), F32), vmem((2, 16, 144, 128), BF16),
            vmem((8, 256, 256), F32), vmem((256, 2048), BF16),
            vmem((8, 144, 128), BF16), vmem((8, 144, 128), BF16), vmem((128, 128), F32),
            vmem((8, 144, 128), BF16), vmem((1024, 256), BF16),
            vmem((4, 512, 128), F32), vmem((4, 512, 128), F32),
            vmem((8, 272, 128), BF16), vmem((8, 272, 128), BF16), vmem((256, 128), F32), vmem((4096, 128), BF16),
            dma((2,)), dma((2, 2)), dma((8,)), dma(()), dma((8, 2)),
            *[dma((2, 8)) for _ in range(8)], *[dma((8,)) for _ in range(4)],
            *[dma((4,)) for _ in range(2)], *[dma((8,)) for _ in range(6)],
        ],
        compiler_params=pltpu.CompilerParams(
            collective_id=0, has_side_effects=True, vmem_limit_bytes=56 * 1024 * 1024),
    )(activations.reshape(br_here * toks, width), out_grads.reshape(br_here * toks, width),
      proj_in, proj_out, fisher_inv, store, lengths, judge_ids.reshape(1, -1))
    return sums.astype(F32)


def solution(mesh):
    placed = (
        P(("grp", "col"), None, "row"),
        P(("grp", "col"), None, "row"),
        P("row", None),
        P("row", None),
        P("row", ("grp", "col")),
        P("row", ("grp", "col")),
        P(("grp", "col")),
        P(),
    )
    return jax.shard_map(
        local, mesh=mesh, in_specs=placed, out_specs=P("row", None), check_vma=False
    )
```

time: 475 us -> 72.9 us (0.15)
  waiting for transfers between devices: 319 us -> 0 us
  blocking collectives: 103 us -> 0 us
  Pallas kernels: 0 us -> 70 us
  matrix products: 34.2 us -> 0 us
  between operations: 13.1 us -> 0.01 us
    psum x2 -> x0, waiting for transfers between devices: 224 us -> none  [the longest x1 149 us: local(): scores = lax.psum(scores_part, ('grp', 'col'))]
    all_gather x1 -> x0, waiting for transfers between devices: 94.9 us -> none  [local(): pre_all = lax.all_gather(pre_rows, 'row', axis=0, tiled=True)]
    psum x1 -> x0, blocking collectives: 74.6 us -> none  [local(): pre_rows = lax.psum(partial_value, ('grp', 'col')).astype(jnp.bfloat16)]
    pallas_call x0 -> x1, Pallas kernels: none -> 70 us  [local(): pl.pallas_call(kernel, out_shape=jax.ShapeDtypeStruct((4096, 128), BF16),...]
    dot_general x6 -> x0, matrix products: 34.2 us -> none  [the longest x1 10.6 us: local(): lax.dot_general(fisher_inv, grad_block, (((1,), (1,)), ((), ())), precisi...]
    all_to_all x1 -> x0, blocking collectives: 28.9 us -> none  [local(): lax.all_to_all(grads, ('grp', 'col'), split_axis=1, concat_axis=0, tiled=...]
  transfers between devices with their start and end apart: 3 -> 0, of which waited for: 3 -> 0; matrix products, arithmetic and copies ran while one was open for 0% -> 0% of each run, Pallas kernels for 0% -> 0%
where the time goes in v2:
time: 72.9 us; the launch traced here: 72.7 us
  Pallas kernels  70 us (96%)
  other arithmetic  2.68 us (4%)
    pallas_call x1, Pallas kernels, local(): pl.pallas_call(kernel, out_shape=jax.ShapeDtypeStruct((4096, 128), BF16),...  70 us
    convert_element_type x1, other arithmetic, local(): return sums.astype(F32)  2.68 us

profile of v2, /device:TPU:1, one launch (start us, length us, event | category | flops | bytes accessed | tf_op | source)
XLA Modules:
  0.0 72.7 jit_solution(11093979133137739729)
XLA Ops:
  0.0 70.0 %shard_map.82 = bf16[4096,128]{1,0:T(8,128)(2,1)} custom-call(bf16[1024,1024]{1,0:T(8,128)(2,1)} %bitcast.3, bf16[1024,1024]{1,0:T(8,128)(2,1)} %bitcast.4, bf16[1024,128]{1,0:T(8,128)(2,1)} %pin.1, bf16[1024,128]{1,0:T(8,128)(2,1)} %pout.1, f32[2048,1024]{1,0:T(8,128)} %fish.1, bf16[4096,1024]{1,0:T(8,128)(2,1)} %store.1, s32[16]{0:T(128)} %lens.1, ...), custom_call_target="tpu_custom_call" | custom-call | tf_op jit(solution)/shard_map/pallas_call | solution.py:383
  70.0 2.7 %convert_element_type.3 = f32[4096,128]{1,0:T(8,128)} convert(bf16[4096,128]{1,0:T(8,128)(2,1)} %shard_map.82) | non-fusion elementwise | flops 524288 | bytes 3145728 | tf_op jit(solution)/shard_map/convert_element_type | solution.py:406

commit v3 on v2

--- a/solution.py
+++ b/solution.py
@@ -6,6 +6,8 @@
 from jax.sharding import PartitionSpec as P
 
 MESH = pl.DeviceIdType.MESH
+SENDS = (6, 5, 7, 2, 4, 1, 3)
+WAITS = (1, 3, 4, 2, 5, 7, 6)
 F32 = jnp.float32
 BF16 = jnp.bfloat16
 SPAN = 80.0
@@ -56,11 +58,11 @@
 
 
 def kernel(
-    act, og, pin, pout, fish, store, lens, ids, out,
-    actv, ogv, pinv, poutv, fv, fhi, flo, sv,
+    act, og, pin, pout, fish, store, lens_in, ids_in, out,
+    lens, ids, actv, ogv, pinv, poutv, fv, fhi, flo, sv,
     proj, p1s, p1r, acc1, p2s, p2r, p3, gf, amat,
-    p4s, p4r, acc4, p5, pre, p6s, p6r, p7s, p7r, acc7, ob,
-    ldw, ld1, ldf, lds, ldo,
+    p4s, p4r, acc4, p5, pre, p6s, p6r, xs, p7s, p7r, acc7, ob,
+    ldi, ldw, ld1, ldf, lds, ldo,
     p1ss, p1rs, p2ss, p2rs, p3ss, p3rs, f3ss, f3rs, p4ss, p4rs, p5ss, p5rs,
     p6ss, p6rs, p7ss, p7rs, p8ss, p8rs, f8ss, f8rs,
 ):
@@ -100,13 +102,17 @@
     load_tokens(0, 0).start()
     load_w[1].start()
     load_tokens(0, 1).start()
-    load_tokens(1, 0).start()
-    load_tokens(1, 1).start()
     barrier = pltpu.get_barrier_semaphore()
     for k in peers:
         pl.semaphore_signal(barrier, inc=1, device_id=to_row[k], device_id_type=MESH)
         pl.semaphore_signal(barrier, inc=1, device_id=to_chip[k], device_id_type=MESH)
     pl.semaphore_signal(barrier, inc=1, device_id=to_sib, device_id_type=MESH)
+    load_tokens(1, 0).start()
+    load_tokens(1, 1).start()
+    load_lens = pltpu.make_async_copy(lens_in, lens, ldi.at[0])
+    load_ids = pltpu.make_async_copy(ids_in, ids, ldi.at[1])
+    load_lens.start()
+    load_ids.start()
 
     def f_load(i):
         rows = pl.ds(pl.multiple_of(i * 256, 256), 256)
@@ -135,14 +141,22 @@
             load_w[1].wait()
         load_tokens(h, 1).wait()
         proj[:, 128:256] = dot(ogv[rows, :], poutv[...])
-        for k in peers:
-            pack(p1s.at[h, k], proj[pl.ds(pl.multiple_of(row_to[k] * 64, 64), 64), :])
-            if h == 0 and k == 1:
+        for k in SENDS:
+            x = proj[pl.ds(pl.multiple_of(row_to[k] * 64, 64), 64), :]
+            m = bound(x)
+            code = encode(x, m.astype(F32))
+            p1s[h, k, 0:64] = code[:, 0:128]
+            p1s[h, k, 64:128] = code[:, 128:256]
+            p1s[h, k, 128:144] = jnp.concatenate(
+                [jnp.broadcast_to(m[:, 0:128], (8, 128)), jnp.broadcast_to(m[:, 128:256], (8, 128))], axis=0)
+            if h == 0 and k == SENDS[0]:
                 pl.semaphore_wait(barrier, 15)
             p1_copy(h, k).start()
         acc1[h] = proj[pl.ds(pl.multiple_of(r * 64, 64), 64), :]
 
     loop(0, 8, lambda i: f_load(i).start())
+    load_lens.wait()
+    load_ids.wait()
     onehot = (lax.broadcasted_iota(jnp.int32, (128, 256), 0) == ids[...]).astype(F32).astype(BF16)
     place = (lax.broadcasted_iota(jnp.int32, (256, 256), 0), lax.broadcasted_iota(jnp.int32, (256, 256), 1))
     moved = lax.rem(lax.div(place[1], 8), 16) * 16 + lax.div(place[1], 128) * 8 + lax.rem(place[1], 8)
@@ -159,9 +173,11 @@
         return remote(p2s.at[h, rows, :], p2r.at[h, rows, :], p2ss.at[h, k], p2rs.at[h, k], to_row[k])
 
     for h in both:
-        for k in peers:
+        for k in WAITS:
             p1_copy(h, k).wait_recv()
-            acc1[h] += unpack(p1r.at[h, k])
+            m = p1r[h, k, 128:144].astype(F32)
+            acc1[h, :, 0:128] += decode(p1r[h, k, 0:64], m[0:1])
+            acc1[h, :, 128:256] += decode(p1r[h, k, 64:128], m[8:9])
         total = acc1[h]
         live = lax.broadcasted_iota(jnp.int32, (64, 128), 0) < lens[8 * h + r]
         ahi, alo = split(total[:, 0:128])
@@ -169,7 +185,7 @@
         p2s[h] = lax.dot_general(
             jnp.concatenate([ghi, ghi, glo], axis=0), jnp.concatenate([ahi, alo, ahi], axis=0),
             (((0,), (0,)), ((), ())), preferred_element_type=F32)
-        for k in peers:
+        for k in SENDS:
             p2_copy(h, k).start()
         own = pl.ds(pl.multiple_of(r * 16, 16), 16)
         p2r[h, own, :] = p2s[h, own, :]
@@ -203,16 +219,16 @@
         for k in peers:
             p2_arrive(h, k).wait_recv()
         pack(p3.at[h, mine3], jnp.concatenate([p2r[h, pl.ds(o, 8, stride=16), :] for o in range(16)], axis=0))
-        for k in peers:
+        for k in SENDS:
             p3_copy(h, k).start()
         p3_onward(h, 0, core).start()
         use3(h, mine3)
     for h in both:
-        for k in peers:
+        for k in WAITS:
             p3_arrive(h, k).wait_recv()
             p3_onward(h, k, core).start()
             use3(h, slot3(chip_from[k], core))
-        for k in range(8):
+        for k in (0, *WAITS):
             p3_onward(h, k, 1 - core).wait_recv()
             use3(h, slot3(chip_from[k], 1 - core))
 
@@ -230,7 +246,7 @@
         return remote(p4s.at[src], p4r.at[src], p4ss.at[src], p4rs.at[src], to_row[k])
 
     def precondition(k):
-        p = lax.rem(lax.div(r, 2) + k, 4)
+        p = lax.rem(rx + 1 - lax.rem(k, 2), 2) * 2 + lax.rem(lax.div(rz, 2) + 1 - lax.div(k, 2), 2)
         lanes = pl.ds(pl.multiple_of(p * 256, 256), 256)
         two = dot(amat[...], fhi[:, lanes])
         full = two[0:128] + two[128:256] + dot(amat[0:128, :], flo[:, lanes])
@@ -246,9 +262,9 @@
             @pl.when(dest == r)
             def _():
                 acc4[...] = part
-    loop(1, 5, precondition)
-
-    for k in peers:
+    loop(0, 4, precondition)
+
+    for k in WAITS:
         p4_arrive(k).wait_recv()
         acc4[...] += unpack(p4r.at[row_from[k]])
 
@@ -266,7 +282,7 @@
 
     own5 = acc4[...].T
     pack(p5.at[r], own5)
-    for k in peers:
+    for k in (2, 1, 3, 6, 5, 7, 4):
         p5_copy(k).start()
     use5(r, own5)
     store_copy.wait()
@@ -274,50 +290,56 @@
         for h in both:
             p1_copy(h, k).wait_send()
             p2_copy(h, k).wait_send()
-    for k in peers:
+    def score(half, group, part):
+        rows = pl.ds(pl.multiple_of(half * 2048 + group * 1024, 1024), 1024)
+        feats = pl.ds(pl.multiple_of(part * 512, 512), 512)
+        two = dot(sv[rows, feats], pre[feats, :])
+        return two[:, 0:128] + two[:, 128:256]
+
+    for k in (1, 3, 2):
         p5_arrive(k).wait_recv()
         use5(row_from[k], unpack(p5.at[row_from[k]]))
 
-    def score(half, pair):
-        rows = pl.ds(pl.multiple_of(half * 2048 + pair * 512, 512), 512)
-        two = dot(sv[rows, :], pre[...])
-        return two[:, 0:128] + two[:, 128:256]
-
-    def p6_copy(t):
-        return remote(p6s.at[t], p6r.at[t], p6ss.at[t], p6rs.at[t], to_sib)
-
-    def p6_send(k):
-        t = lax.rem(lax.div(q, 2) + k, 4)
-        p6s[t] = score(1 - core, t)
-        p6_copy(t).start()
-    loop(1, 5, p6_send)
-
-    def p7_copy(dest):
-        return remote(p7s.at[dest], p7r.at[q], p7ss.at[dest], p7rs.at[q],
-                      {"grp": lax.div(dest, 4), "col": lax.rem(dest, 4) * 2 + core})
-
-    def p7_arrive(k):
-        src = chip_from[k]
-        return remote(p7s.at[src], p7r.at[src], p7ss.at[src], p7rs.at[src], to_chip[k])
-
-    def p7_send(k):
-        t = lax.rem(lax.div(q, 2) + k, 4)
-        x = score(core, t)
-        p6_copy(t).wait_recv()
-        x = x + p6r[t]
-        for e in both:
-            dest = 2 * t + e
-            part = x[256 * e:256 * e + 256]
-            pack(p7s.at[dest], part)
-
-            @pl.when(dest != q)
-            def _():
-                p7_copy(dest).start()
-
-            @pl.when(dest == q)
-            def _():
-                acc7[...] = part
-    loop(1, 5, p7_send)
+    def score_own(u):
+        p6s[u] = score(1 - core, u, rx)
+        xs[u] = score(core, u, rx)
+    loop(0, 2, score_own)
+    for k in (4, 5, 7, 6):
+        p5_arrive(k).wait_recv()
+        use5(row_from[k], unpack(p5.at[row_from[k]]))
+
+    def p6_copy(u):
+        return remote(p6s.at[u], p6r.at[u], p6ss.at[u], p6rs.at[u], to_sib)
+
+    def p6_send(i):
+        u = lax.rem(g + 1 + i, 2)
+        p6s[u] += score(1 - core, u, 1 - rx)
+        p6_copy(u).start()
+    loop(0, 2, p6_send)
+
+    parts = (pl.ds(0, 144), pl.ds(144, 128))
+
+    def p7_copy(k, a):
+        return remote(p7s.at[k, parts[a]], p7r.at[k, parts[a]], p7ss.at[k, a], p7rs.at[k, a], to_chip[k])
+
+    for i in both:
+        u = lax.rem(g + 1 + i, 2)
+        xs[u] += score(core, u, 1 - rx)
+        p6_copy(u).wait_recv()
+        for k in ((6, 5, 7, 4), (2, 1, 3, 0))[i]:
+            rows = pl.ds(pl.multiple_of(lax.rem(chip_to[k], 4) * 256, 256), 256)
+            x = xs[u, rows, :] + p6r[u, rows, :]
+            if k == 0:
+                acc7[...] = x
+                continue
+            m = bound(x)
+            code = encode(x, m.astype(F32))
+            p7s[k, 0:128] = code[0:128]
+            p7s[k, 128:144] = jnp.broadcast_to(m, (16, 128))
+            p7s[k, 144:272] = code[128:256]
+            p7_copy(k, 0).start()
+    for k in SENDS:
+        p7_copy(k, 1).start()
 
     for k in peers:
         p4_copy(row_to[k]).wait_send()
@@ -328,51 +350,75 @@
         for h in both:
             p3_onward(h, k, core).wait_send()
 
+    def place8(chip, which, a):
+        return pl.ds(pl.multiple_of(which * 2048 + chip * 256 + a * 128, 128), 128)
+
+    def p8_copy(k, a):
+        rows = place8(q, core, a)
+        return remote(ob.at[rows, :], ob.at[rows, :], p8ss.at[k, a], p8rs.at[k, a], to_chip[k])
+
+    def p8_arrive(k, a):
+        rows = place8(chip_from[k], core, a)
+        return remote(ob.at[rows, :], ob.at[rows, :], p8ss.at[k, a], p8rs.at[k, a], to_chip[k])
+
+    def p8_onward(k, which, a):
+        rows = place8(chip_from[k], which, a)
+        return remote(ob.at[rows, :], out.at[rows, :], f8ss.at[k, a], f8rs.at[k, a], to_sib)
+
+    def leave(k, a):
+        rows = place8(chip_from[k], core, a)
+        return pltpu.make_async_copy(ob.at[rows, :], out.at[rows, :], ldo.at[k, a])
+
+    for a in both:
+        half = slice(128 * a, 128 * a + 128)
+        for k in WAITS:
+            p7_copy(k, a).wait_recv()
+            acc7[half] += decode(p7r[k, parts[a]][0:128], p7r[k, 128:144][:1].astype(F32))
+        ob[place8(q, core, a), :] = acc7[half].astype(BF16)
+        for k in SENDS:
+            p8_copy(k, a).start()
+        p8_onward(0, core, a).start()
+        leave(0, a).start()
     for k in peers:
-        p7_arrive(k).wait_recv()
-        acc7[...] += unpack(p7r.at[chip_from[k]])
-
-    def place8(chip, which):
-        return pl.ds(pl.multiple_of(which * 2048 + chip * 256, 256), 256)
-
-    mine8 = place8(q, core)
-    ob[mine8, :] = acc7[...].astype(BF16)
-
-    def p8_copy(k):
-        return remote(ob.at[mine8, :], ob.at[mine8, :], p8ss.at[k], p8rs.at[k], to_chip[k])
-
-    def p8_arrive(k):
-        rows = place8(chip_from[k], core)
-        return remote(ob.at[rows, :], ob.at[rows, :], p8ss.at[k], p8rs.at[k], to_chip[k])
-
-    def p8_onward(k, which):
-        rows = place8(chip_from[k], which)
-        return remote(ob.at[rows, :], ob.at[rows, :], f8ss.at[k], f8rs.at[k], to_sib)
-
-    def leave(k, which):
-        rows = place8(chip_from[k], which)
-        return pltpu.make_async_copy(ob.at[rows, :], out.at[rows, :], ldo.at[k, which])
-
-    for k in peers:
-        p8_copy(k).start()
-    p8_onward(0, core).start()
-    leave(0, core).start()
-    for k in peers:
-        p7_copy(chip_to[k]).wait_send()
-    loop(0, 4, lambda t: p6_copy(t).wait_send())
-    for k in peers:
-        p8_arrive(k).wait_recv()
-        p8_onward(k, core).start()
-        leave(k, core).start()
-    for k in range(8):
-        p8_onward(k, 1 - core).wait_recv()
-        leave(k, 1 - core).start()
-    for k in peers:
-        p8_copy(k).wait_send()
-    for k in range(8):
-        p8_onward(k, core).wait_send()
-        leave(k, core).wait()
-        leave(k, 1 - core).wait()
+        for a in both:
+            p7_copy(k, a).wait_send()
+    loop(0, 2, lambda u: p6_copy(u).wait_send())
+    for a in both:
+        for k in WAITS:
+            p8_arrive(k, a).wait_recv()
+            p8_onward(k, core, a).start()
+            leave(k, a).start()
+    for a in both:
+        for k in peers:
+            p8_copy(k, a).wait_send()
+        for k in range(8):
+            p8_onward(k, core, a).wait_send()
+            leave(k, a).wait()
+    for a in both:
+        for k in range(8):
+            p8_onward(k, 1 - core, a).wait_recv()
+
+
+def widen(src, dst, held, wide, got, put):
+    count = got.shape[0]
+    rows = src.shape[0] // count
+
+    def load(i):
+        part = pl.ds(i * rows, rows)
+        return pltpu.make_async_copy(src.at[part, :], held.at[part, :], got.at[i])
+
+    def leave(i):
+        part = pl.ds(i * rows, rows)
+        return pltpu.make_async_copy(wide.at[part, :], dst.at[part, :], put.at[i])
+
+    for i in range(count):
+        load(i).start()
+    for i in range(count):
+        load(i).wait()
+        wide[i * rows:(i + 1) * rows] = held[i * rows:(i + 1) * rows].astype(F32)
+        leave(i).start()
+    for i in range(count):
+        leave(i).wait()
 
 
 def local(activations, out_grads, proj_in, proj_out, fisher_inv, store, lengths, judge_ids):
@@ -383,27 +429,33 @@
     sums = pl.pallas_call(
         kernel,
         out_shape=jax.ShapeDtypeStruct((4096, 128), BF16),
-        in_specs=[any_spec] * 6 + [pl.BlockSpec(memory_space=pltpu.SMEM), pl.BlockSpec(memory_space=pltpu.VMEM)],
+        in_specs=[any_spec] * 8,
         out_specs=any_spec,
         scratch_shapes=[
-            vmem((1024, 1024), BF16), vmem((1024, 1024), BF16), vmem((1024, 128), BF16), vmem((1024, 128), BF16),
+            pltpu.SMEM((16,), jnp.int32), vmem((1, 256), jnp.int32), vmem((1024, 1024), BF16), vmem((1024, 1024), BF16), vmem((1024, 128), BF16), vmem((1024, 128), BF16),
             vmem((2048, 1024), F32), vmem((2048, 1024), BF16), vmem((2048, 1024), BF16), vmem((4096, 1024), BF16),
-            vmem((512, 256), F32), vmem((2, 8, 80, 256), BF16), vmem((2, 8, 80, 256), BF16), vmem((2, 64, 256), F32),
+            vmem((512, 256), F32), vmem((2, 8, 144, 128), BF16), vmem((2, 8, 144, 128), BF16), vmem((2, 64, 256), F32),
             vmem((2, 128, 128), F32), vmem((2, 128, 128), F32), vmem((2, 16, 144, 128), BF16),
             vmem((8, 256, 256), F32), vmem((256, 2048), BF16),
             vmem((8, 144, 128), BF16), vmem((8, 144, 128), BF16), vmem((128, 128), F32),
             vmem((8, 144, 128), BF16), vmem((1024, 256), BF16),
-            vmem((4, 512, 128), F32), vmem((4, 512, 128), F32),
+            vmem((2, 1024, 128), F32), vmem((2, 1024, 128), F32), vmem((2, 1024, 128), F32),
             vmem((8, 272, 128), BF16), vmem((8, 272, 128), BF16), vmem((256, 128), F32), vmem((4096, 128), BF16),
-            dma((2,)), dma((2, 2)), dma((8,)), dma(()), dma((8, 2)),
+            dma((2,)), dma((2,)), dma((2, 2)), dma((8,)), dma(()), dma((8, 2)),
             *[dma((2, 8)) for _ in range(8)], *[dma((8,)) for _ in range(4)],
-            *[dma((4,)) for _ in range(2)], *[dma((8,)) for _ in range(6)],
+            *[dma((2,)) for _ in range(2)], *[dma((8, 2)) for _ in range(6)],
         ],
         compiler_params=pltpu.CompilerParams(
             collective_id=0, has_side_effects=True, vmem_limit_bytes=56 * 1024 * 1024),
     )(activations.reshape(br_here * toks, width), out_grads.reshape(br_here * toks, width),
       proj_in, proj_out, fisher_inv, store, lengths, judge_ids.reshape(1, -1))
-    return sums.astype(F32)
+    return pl.pallas_call(
+        widen,
+        out_shape=jax.ShapeDtypeStruct((4096, 128), F32),
+        in_specs=[any_spec],
+        out_specs=any_spec,
+        scratch_shapes=[vmem((4096, 128), BF16), vmem((4096, 128), F32), dma((8,)), dma((8,))],
+    )(sums)
 
 
 def solution(mesh):

time: 72.9 us -> 68.7 us (0.942)
  other arithmetic: 2.68 us -> 0 us
  Pallas kernels: 70 us -> 68.6 us
    pallas_call x1, Pallas kernels: 70 us -> 66.2 us  [local(): pl.pallas_call(kernel, out_shape=jax.ShapeDtypeStruct((4096, 128), BF16),...]
    convert_element_type x1 -> x0, other arithmetic: 2.68 us -> none  [local(): return sums.astype(F32)]
    pallas_call x0 -> x1, Pallas kernels: none -> 2.37 us  [local(): pl.pallas_call(widen, out_shape=jax.ShapeDtypeStruct((4096, 128), F32), i...]
where the time goes in v3:
time: 68.7 us; the launch traced here: 68.6 us
  Pallas kernels  68.6 us (100%)
    pallas_call x1, Pallas kernels, local(): pl.pallas_call(kernel, out_shape=jax.ShapeDtypeStruct((4096, 128), BF16),...  66.2 us
    pallas_call x1, Pallas kernels, local(): pl.pallas_call(widen, out_shape=jax.ShapeDtypeStruct((4096, 128), F32), i...  2.37 us

profile of v3, /device:TPU:1, one launch (start us, length us, event | category | flops | bytes accessed | tf_op | source)
XLA Modules:
  0.0 68.6 jit_solution(15082095062356603378)
XLA Ops:
  0.0 66.2 %shard_map.82.src = bf16[4096,128]{1,0:T(8,128)(2,1)} custom-call(bf16[1024,1024]{1,0:T(8,128)(2,1)} %bitcast.3, bf16[1024,1024]{1,0:T(8,128)(2,1)} %bitcast.4, bf16[1024,128]{1,0:T(8,128)(2,1)} %pin.1, bf16[1024,128]{1,0:T(8,128)(2,1)} %pout.1, f32[2048,1024]{1,0:T(8,128)} %fish.1, bf16[4096,1024]{1,0:T(8,128)(2,1)} %store.1, s32[16]{0:T(128)} %lens_in.1, ...), custom_call_target="tpu_custom_call" | custom-call | tf_op jit(solution)/shard_map/pallas_call | solution.py:429
  66.2 2.4 %shard_map.83 = f32[4096,128]{1,0:T(8,128)} custom-call(bf16[4096,128]{1,0:T(8,128)(2,1)} %shard_map.82.src), custom_call_target="tpu_custom_call" | custom-call | tf_op jit(solution)/shard_map/pallas_call | solution.py:452

commit v4 on v3

--- a/solution.py
+++ b/solution.py
@@ -193,44 +193,49 @@
     store_copy.start()
     loop(5, 8, f_split)
 
-    def slot3(chip, k):
-        return chip * 2 + k
-
-    mine3 = slot3(q, core)
-
     def p3_copy(h, k):
-        return remote(p3.at[h, mine3], p3.at[h, mine3], p3ss.at[h, k], p3rs.at[h, k], to_chip[k])
+        return remote(p3.at[h, q, core], p3.at[h, q, core], p3ss.at[h, k], p3rs.at[h, k], to_chip[k])
 
     def p3_arrive(h, k):
-        slot = slot3(chip_from[k], core)
-        return remote(p3.at[h, slot], p3.at[h, slot], p3ss.at[h, k], p3rs.at[h, k], to_chip[k])
-
-    def p3_onward(h, k, which):
-        slot = slot3(chip_from[k], which)
-        return remote(p3.at[h, slot], p3.at[h, slot], f3ss.at[h, k], f3rs.at[h, k], to_sib)
-
-    def use3(h, slot):
-        x = unpack(p3.at[h, slot])
-        rows = pl.ds(pl.multiple_of(h * 128 + slot * 8, 8), 8)
+        spot = p3.at[h, chip_from[k], core]
+        return remote(spot, spot, p3ss.at[h, k], p3rs.at[h, k], to_chip[k])
+
+    def p3_onward(k, which):
+        spot = p3.at[1, chip_from[k], which]
+        return remote(spot, spot, f3ss.at[1, k], f3rs.at[1, k], to_sib)
+
+    def p3_onward_all(which):
+        return remote(p3.at[0, :, which], p3.at[0, :, which], f3ss.at[0, 0], f3rs.at[0, 0], to_sib)
+
+    def use3(h, chip, which):
+        x = unpack(p3.at[h, chip, which])
+        rows = pl.ds(pl.multiple_of(h * 128 + chip * 16 + which * 8, 8), 8)
         for o in range(16):
             gf[o // 2, rows, (o % 2) * 128:(o % 2) * 128 + 128] = x[8 * o:8 * o + 8]
 
     for h in both:
         for k in peers:
             p2_arrive(h, k).wait_recv()
-        pack(p3.at[h, mine3], jnp.concatenate([p2r[h, pl.ds(o, 8, stride=16), :] for o in range(16)], axis=0))
+        pack(p3.at[h, q, core],
+             jnp.concatenate([p2r[h, pl.ds(o, 8, stride=16), :] for o in range(16)], axis=0))
         for k in SENDS:
             p3_copy(h, k).start()
-        p3_onward(h, 0, core).start()
-        use3(h, mine3)
-    for h in both:
-        for k in WAITS:
-            p3_arrive(h, k).wait_recv()
-            p3_onward(h, k, core).start()
-            use3(h, slot3(chip_from[k], core))
-        for k in (0, *WAITS):
-            p3_onward(h, k, 1 - core).wait_recv()
-            use3(h, slot3(chip_from[k], 1 - core))
+        use3(h, q, core)
+    for k in WAITS:
+        p3_arrive(0, k).wait_recv()
+        use3(0, chip_from[k], core)
+    p3_onward_all(core).start()
+    p3_onward(0, core).start()
+    for k in WAITS:
+        p3_arrive(1, k).wait_recv()
+        p3_onward(k, core).start()
+        use3(1, chip_from[k], core)
+    p3_onward_all(1 - core).wait_recv()
+    for k in (0, *WAITS):
+        use3(0, chip_from[k], 1 - core)
+    for k in (0, *WAITS):
+        p3_onward(k, 1 - core).wait_recv()
+        use3(1, chip_from[k], 1 - core)
 
     for j in range(8):
         hi, lo = split(gf[j])
@@ -308,13 +313,15 @@
         p5_arrive(k).wait_recv()
         use5(row_from[k], unpack(p5.at[row_from[k]]))
 
-    def p6_copy(u):
-        return remote(p6s.at[u], p6r.at[u], p6ss.at[u], p6rs.at[u], to_sib)
+    def p6_copy(i, kk):
+        spot = (lax.rem(g + 1 + i, 2), pl.ds(pl.multiple_of(lax.rem(y + kk, 4) * 256, 256), 256))
+        return remote(p6s.at[spot], p6r.at[spot], p6ss.at[i, kk], p6rs.at[i, kk], to_sib)
 
     def p6_send(i):
         u = lax.rem(g + 1 + i, 2)
         p6s[u] += score(1 - core, u, 1 - rx)
-        p6_copy(u).start()
+        for kk in (2, 1, 3, 0):
+            p6_copy(i, kk).start()
     loop(0, 2, p6_send)
 
     parts = (pl.ds(0, 144), pl.ds(144, 128))
@@ -322,22 +329,33 @@
     def p7_copy(k, a):
         return remote(p7s.at[k, parts[a]], p7r.at[k, parts[a]], p7ss.at[k, a], p7rs.at[k, a], to_chip[k])
 
-    for i in both:
+    def p7_first(i):
         u = lax.rem(g + 1 + i, 2)
         xs[u] += score(core, u, 1 - rx)
-        p6_copy(u).wait_recv()
-        for k in ((6, 5, 7, 4), (2, 1, 3, 0))[i]:
-            rows = pl.ds(pl.multiple_of(lax.rem(chip_to[k], 4) * 256, 256), 256)
+        for kk in (2, 1, 3, 0):
+            p6_copy(i, kk).wait_recv()
+            k = 4 - 4 * i + kk
+            there = lax.rem(y + kk, 4)
+            rows = pl.ds(pl.multiple_of(there * 256, 256), 256)
             x = xs[u, rows, :] + p6r[u, rows, :]
-            if k == 0:
-                acc7[...] = x
-                continue
             m = bound(x)
             code = encode(x, m.astype(F32))
             p7s[k, 0:128] = code[0:128]
             p7s[k, 128:144] = jnp.broadcast_to(m, (16, 128))
             p7s[k, 144:272] = code[128:256]
-            p7_copy(k, 0).start()
+            send = remote(p7s.at[k, parts[0]], p7r.at[k, parts[0]], p7ss.at[k, 0], p7rs.at[k, 0],
+                          {"grp": u, "col": there * 2 + core})
+            if kk:
+                send.start()
+            else:
+                @pl.when(i == 0)
+                def _():
+                    send.start()
+
+                @pl.when(i == 1)
+                def _():
+                    acc7[...] = x
+    loop(0, 2, p7_first)
     for k in SENDS:
         p7_copy(k, 1).start()
 
@@ -346,57 +364,62 @@
         p5_copy(k).wait_send()
         for h in both:
             p3_copy(h, k).wait_send()
+    p3_onward_all(core).wait_send()
     for k in range(8):
-        for h in both:
-            p3_onward(h, k, core).wait_send()
-
-    def place8(chip, which, a):
-        return pl.ds(pl.multiple_of(which * 2048 + chip * 256 + a * 128, 128), 128)
+        p3_onward(k, core).wait_send()
 
     def p8_copy(k, a):
-        rows = place8(q, core, a)
-        return remote(ob.at[rows, :], ob.at[rows, :], p8ss.at[k, a], p8rs.at[k, a], to_chip[k])
+        rows = pl.ds(128 * a, 128)
+        return remote(ob.at[core, q, rows], ob.at[core, q, rows], p8ss.at[k, a], p8rs.at[k, a], to_chip[k])
 
     def p8_arrive(k, a):
-        rows = place8(chip_from[k], core, a)
-        return remote(ob.at[rows, :], ob.at[rows, :], p8ss.at[k, a], p8rs.at[k, a], to_chip[k])
-
-    def p8_onward(k, which, a):
-        rows = place8(chip_from[k], which, a)
-        return remote(ob.at[rows, :], out.at[rows, :], f8ss.at[k, a], f8rs.at[k, a], to_sib)
-
-    def leave(k, a):
-        rows = place8(chip_from[k], core, a)
-        return pltpu.make_async_copy(ob.at[rows, :], out.at[rows, :], ldo.at[k, a])
+        rows = pl.ds(128 * a, 128)
+        spot = ob.at[core, chip_from[k], rows]
+        return remote(spot, spot, p8ss.at[k, a], p8rs.at[k, a], to_chip[k])
+
+    def p8_onward(k, which):
+        rows = pl.ds(128, 128)
+        return remote(ob.at[which, chip_from[k], rows], out.at[which, chip_from[k], rows], f8ss.at[k, 1], f8rs.at[k, 1],
+                      to_sib)
+
+    def p8_onward_all(which):
+        rows = pl.ds(0, 128)
+        return remote(ob.at[which, :, rows], out.at[which, :, rows], f8ss.at[0, 0], f8rs.at[0, 0], to_sib)
 
     for a in both:
         half = slice(128 * a, 128 * a + 128)
         for k in WAITS:
             p7_copy(k, a).wait_recv()
             acc7[half] += decode(p7r[k, parts[a]][0:128], p7r[k, 128:144][:1].astype(F32))
-        ob[place8(q, core, a), :] = acc7[half].astype(BF16)
+        ob[core, q, half] = acc7[half].astype(BF16)
         for k in SENDS:
             p8_copy(k, a).start()
-        p8_onward(0, core, a).start()
-        leave(0, a).start()
     for k in peers:
         for a in both:
             p7_copy(k, a).wait_send()
-    loop(0, 2, lambda u: p6_copy(u).wait_send())
-    for a in both:
-        for k in WAITS:
-            p8_arrive(k, a).wait_recv()
-            p8_onward(k, core, a).start()
-            leave(k, a).start()
-    for a in both:
-        for k in peers:
-            p8_copy(k, a).wait_send()
-        for k in range(8):
-            p8_onward(k, core, a).wait_send()
-            leave(k, a).wait()
-    for a in both:
-        for k in range(8):
-            p8_onward(k, 1 - core, a).wait_recv()
+    for i in both:
+        for kk in range(4):
+            p6_copy(i, kk).wait_send()
+    for k in WAITS:
+        p8_arrive(k, 0).wait_recv()
+    p8_onward_all(core).start()
+    p8_onward(0, core).start()
+    for k in peers:
+        p8_copy(k, 0).wait_send()
+    for k in WAITS:
+        p8_arrive(k, 1).wait_recv()
+        p8_onward(k, core).start()
+    leave = pltpu.make_async_copy(ob.at[core], out.at[core], ldo)
+    leave.start()
+    for k in peers:
+        p8_copy(k, 1).wait_send()
+    p8_onward_all(core).wait_send()
+    p8_onward_all(1 - core).wait_recv()
+    for k in range(8):
+        p8_onward(k, core).wait_send()
+    for k in range(8):
+        p8_onward(k, 1 - core).wait_recv()
+    leave.wait()
 
 
 def widen(src, dst, held, wide, got, put):
@@ -428,22 +451,22 @@
     vmem = pltpu.VMEM
     sums = pl.pallas_call(
         kernel,
-        out_shape=jax.ShapeDtypeStruct((4096, 128), BF16),
+        out_shape=jax.ShapeDtypeStruct((2, 8, 256, 128), BF16),
         in_specs=[any_spec] * 8,
         out_specs=any_spec,
         scratch_shapes=[
             pltpu.SMEM((16,), jnp.int32), vmem((1, 256), jnp.int32), vmem((1024, 1024), BF16), vmem((1024, 1024), BF16), vmem((1024, 128), BF16), vmem((1024, 128), BF16),
             vmem((2048, 1024), F32), vmem((2048, 1024), BF16), vmem((2048, 1024), BF16), vmem((4096, 1024), BF16),
             vmem((512, 256), F32), vmem((2, 8, 144, 128), BF16), vmem((2, 8, 144, 128), BF16), vmem((2, 64, 256), F32),
-            vmem((2, 128, 128), F32), vmem((2, 128, 128), F32), vmem((2, 16, 144, 128), BF16),
+            vmem((2, 128, 128), F32), vmem((2, 128, 128), F32), vmem((2, 8, 2, 144, 128), BF16),
             vmem((8, 256, 256), F32), vmem((256, 2048), BF16),
             vmem((8, 144, 128), BF16), vmem((8, 144, 128), BF16), vmem((128, 128), F32),
             vmem((8, 144, 128), BF16), vmem((1024, 256), BF16),
             vmem((2, 1024, 128), F32), vmem((2, 1024, 128), F32), vmem((2, 1024, 128), F32),
-            vmem((8, 272, 128), BF16), vmem((8, 272, 128), BF16), vmem((256, 128), F32), vmem((4096, 128), BF16),
-            dma((2,)), dma((2,)), dma((2, 2)), dma((8,)), dma(()), dma((8, 2)),
+            vmem((8, 272, 128), BF16), vmem((8, 272, 128), BF16), vmem((256, 128), F32), vmem((2, 8, 256, 128), BF16),
+            dma((2,)), dma((2,)), dma((2, 2)), dma((8,)), dma(()), dma(()),
             *[dma((2, 8)) for _ in range(8)], *[dma((8,)) for _ in range(4)],
-            *[dma((2,)) for _ in range(2)], *[dma((8, 2)) for _ in range(6)],
+            *[dma((2, 4)) for _ in range(2)], *[dma((8, 2)) for _ in range(6)],
         ],
         compiler_params=pltpu.CompilerParams(
             collective_id=0, has_side_effects=True, vmem_limit_bytes=56 * 1024 * 1024),
@@ -455,7 +478,7 @@
         in_specs=[any_spec],
         out_specs=any_spec,
         scratch_shapes=[vmem((4096, 128), BF16), vmem((4096, 128), F32), dma((8,)), dma((8,))],
-    )(sums)
+    )(sums.reshape(4096, 128))
 
 
 def solution(mesh):

time: 68.7 us -> 68.3 us (level)
  no operation moved by 1% of the time
where the time goes in v4:
time: 68.3 us; the launch traced here: 68.2 us
  Pallas kernels  68.2 us (100%)
    pallas_call x1, Pallas kernels, local(): pl.pallas_call(kernel, out_shape=jax.ShapeDtypeStruct((2, 8, 256, 128), B...  65.8 us
    pallas_call x1, Pallas kernels, local(): pl.pallas_call(widen, out_shape=jax.ShapeDtypeStruct((4096, 128), F32), i...  2.37 us

profile of v4, /device:TPU:1, one launch (start us, length us, event | category | flops | bytes accessed | tf_op | source)
XLA Modules:
  0.0 68.2 jit_solution(9282989232891626722)
XLA Ops:
  0.0 65.8 %shard_map.82 = bf16[2,8,256,128]{3,2,1,0:T(8,128)(2,1)} custom-call(bf16[1024,1024]{1,0:T(8,128)(2,1)} %bitcast.5, bf16[1024,1024]{1,0:T(8,128)(2,1)} %bitcast.6, bf16[1024,128]{1,0:T(8,128)(2,1)} %pin.1, bf16[1024,128]{1,0:T(8,128)(2,1)} %pout.1, f32[2048,1024]{1,0:T(8,128)} %fish.1, bf16[4096,1024]{1,0:T(8,128)(2,1)} %store.1, s32[16]{0:T(128)} %lens_in.1, ...), custom_call_target="tpu_custom_call" | custom-call | tf_op jit(solution)/shard_map/pallas_call | solution.py:452
  65.8 2.4 %shard_map.83 = f32[4096,128]{1,0:T(8,128)} custom-call(bf16[4096,128]{1,0:T(8,128)(2,1)} %bitcast.4), custom_call_target="tpu_custom_call" | custom-call | tf_op jit(solution)/shard_map/pallas_call | solution.py:475

commit v5 on v4

--- a/solution.py
+++ b/solution.py
@@ -63,8 +63,7 @@
     proj, p1s, p1r, acc1, p2s, p2r, p3, gf, amat,
     p4s, p4r, acc4, p5, pre, p6s, p6r, xs, p7s, p7r, acc7, ob,
     ldi, ldw, ld1, ldf, lds, ldo,
-    p1ss, p1rs, p2ss, p2rs, p3ss, p3rs, f3ss, f3rs, p4ss, p4rs, p5ss, p5rs,
-    p6ss, p6rs, p7ss, p7rs, p8ss, p8rs, f8ss, f8rs,
+    p1ss, p1rs, p2ss, p2rs, p3ss, p3rs, f3ss, f3rs, p4rs, p5rs, p6rs, p7rs, p8rs, f8rs,
 ):
     g = lax.axis_index("grp")
     r = lax.axis_index("row")
@@ -221,6 +220,10 @@
         for k in SENDS:
             p3_copy(h, k).start()
         use3(h, q, core)
+    for k in peers:
+        for h in both:
+            p1_copy(h, k).wait_send()
+            p2_copy(h, k).wait_send()
     for k in WAITS:
         p3_arrive(0, k).wait_recv()
         use3(0, chip_from[k], core)
@@ -244,11 +247,11 @@
         amat[128:256, 256 * j:256 * j + 256] = lo
 
     def p4_copy(dest):
-        return remote(p4s.at[dest], p4r.at[r], p4ss.at[dest], p4rs.at[r], {"row": dest})
+        return remote(p4s.at[dest], p4r.at[r], p1ss.at[0, dest], p4rs.at[r], {"row": dest})
 
     def p4_arrive(k):
         src = row_from[k]
-        return remote(p4s.at[src], p4r.at[src], p4ss.at[src], p4rs.at[src], to_row[k])
+        return remote(p4s.at[src], p4r.at[src], p1ss.at[0, src], p4rs.at[src], to_row[k])
 
     def precondition(k):
         p = lax.rem(rx + 1 - lax.rem(k, 2), 2) * 2 + lax.rem(lax.div(rz, 2) + 1 - lax.div(k, 2), 2)
@@ -274,10 +277,10 @@
         acc4[...] += unpack(p4r.at[row_from[k]])
 
     def p5_copy(k):
-        return remote(p5.at[r], p5.at[r], p5ss.at[k], p5rs.at[k], to_row[k])
+        return remote(p5.at[r], p5.at[r], p1ss.at[1, k], p5rs.at[k], to_row[k])
 
     def p5_arrive(k):
-        return remote(p5.at[row_from[k]], p5.at[row_from[k]], p5ss.at[k], p5rs.at[k], to_row[k])
+        return remote(p5.at[row_from[k]], p5.at[row_from[k]], p1ss.at[1, k], p5rs.at[k], to_row[k])
 
     def use5(i, x):
         hi, lo = split(x)
@@ -293,8 +296,10 @@
     store_copy.wait()
     for k in peers:
         for h in both:
-            p1_copy(h, k).wait_send()
-            p2_copy(h, k).wait_send()
+            p3_copy(h, k).wait_send()
+    p3_onward_all(core).wait_send()
+    for k in range(8):
+        p3_onward(k, core).wait_send()
     def score(half, group, part):
         rows = pl.ds(pl.multiple_of(half * 2048 + group * 1024, 1024), 1024)
         feats = pl.ds(pl.multiple_of(part * 512, 512), 512)
@@ -315,7 +320,7 @@
 
     def p6_copy(i, kk):
         spot = (lax.rem(g + 1 + i, 2), pl.ds(pl.multiple_of(lax.rem(y + kk, 4) * 256, 256), 256))
-        return remote(p6s.at[spot], p6r.at[spot], p6ss.at[i, kk], p6rs.at[i, kk], to_sib)
+        return remote(p6s.at[spot], p6r.at[spot], p2ss.at[0, i * 4 + kk], p6rs.at[i, kk], to_sib)
 
     def p6_send(i):
         u = lax.rem(g + 1 + i, 2)
@@ -327,7 +332,7 @@
     parts = (pl.ds(0, 144), pl.ds(144, 128))
 
     def p7_copy(k, a):
-        return remote(p7s.at[k, parts[a]], p7r.at[k, parts[a]], p7ss.at[k, a], p7rs.at[k, a], to_chip[k])
+        return remote(p7s.at[k, parts[a]], p7r.at[k, parts[a]], (p2ss, p3ss)[a].at[1, k], p7rs.at[k, a], to_chip[k])
 
     def p7_first(i):
         u = lax.rem(g + 1 + i, 2)
@@ -343,7 +348,7 @@
             p7s[k, 0:128] = code[0:128]
             p7s[k, 128:144] = jnp.broadcast_to(m, (16, 128))
             p7s[k, 144:272] = code[128:256]
-            send = remote(p7s.at[k, parts[0]], p7r.at[k, parts[0]], p7ss.at[k, 0], p7rs.at[k, 0],
+            send = remote(p7s.at[k, parts[0]], p7r.at[k, parts[0]], p2ss.at[1, k], p7rs.at[k, 0],
                           {"grp": u, "col": there * 2 + core})
             if kk:
                 send.start()
@@ -362,29 +367,24 @@
     for k in peers:
         p4_copy(row_to[k]).wait_send()
         p5_copy(k).wait_send()
-        for h in both:
-            p3_copy(h, k).wait_send()
-    p3_onward_all(core).wait_send()
-    for k in range(8):
-        p3_onward(k, core).wait_send()
 
     def p8_copy(k, a):
         rows = pl.ds(128 * a, 128)
-        return remote(ob.at[core, q, rows], ob.at[core, q, rows], p8ss.at[k, a], p8rs.at[k, a], to_chip[k])
+        return remote(ob.at[core, q, rows], ob.at[core, q, rows], (p3ss, p1ss)[a].at[0, k], p8rs.at[k, a], to_chip[k])
 
     def p8_arrive(k, a):
         rows = pl.ds(128 * a, 128)
         spot = ob.at[core, chip_from[k], rows]
-        return remote(spot, spot, p8ss.at[k, a], p8rs.at[k, a], to_chip[k])
+        return remote(spot, spot, (p3ss, p1ss)[a].at[0, k], p8rs.at[k, a], to_chip[k])
 
     def p8_onward(k, which):
         rows = pl.ds(128, 128)
-        return remote(ob.at[which, chip_from[k], rows], out.at[which, chip_from[k], rows], f8ss.at[k, 1], f8rs.at[k, 1],
+        return remote(ob.at[which, chip_from[k], rows], out.at[which, chip_from[k], rows], f3ss.at[1, k], f8rs.at[k, 1],
                       to_sib)
 
     def p8_onward_all(which):
         rows = pl.ds(0, 128)
-        return remote(ob.at[which, :, rows], out.at[which, :, rows], f8ss.at[0, 0], f8rs.at[0, 0], to_sib)
+        return remote(ob.at[which, :, rows], out.at[which, :, rows], f3ss.at[0, 0], f8rs.at[0, 0], to_sib)
 
     for a in both:
         half = slice(128 * a, 128 * a + 128)
@@ -465,8 +465,7 @@
             vmem((2, 1024, 128), F32), vmem((2, 1024, 128), F32), vmem((2, 1024, 128), F32),
             vmem((8, 272, 128), BF16), vmem((8, 272, 128), BF16), vmem((256, 128), F32), vmem((2, 8, 256, 128), BF16),
             dma((2,)), dma((2,)), dma((2, 2)), dma((8,)), dma(()), dma(()),
-            *[dma((2, 8)) for _ in range(8)], *[dma((8,)) for _ in range(4)],
-            *[dma((2, 4)) for _ in range(2)], *[dma((8, 2)) for _ in range(6)],
+            *[dma((2, 8)) for _ in range(8)], dma((8,)), dma((8,)), dma((2, 4)), *[dma((8, 2)) for _ in range(3)],
         ],
         compiler_params=pltpu.CompilerParams(
             collective_id=0, has_side_effects=True, vmem_limit_bytes=56 * 1024 * 1024),

time: 68.3 us -> 67.7 us (level)
  Pallas kernels: 68.2 us -> 67.5 us
where the time goes in v5:
time: 67.7 us; the launch traced here: 67.5 us
  Pallas kernels  67.5 us (100%)
    pallas_call x1, Pallas kernels, local(): pl.pallas_call(kernel, out_shape=jax.ShapeDtypeStruct((2, 8, 256, 128), B...  65.1 us
    pallas_call x1, Pallas kernels, local(): pl.pallas_call(widen, out_shape=jax.ShapeDtypeStruct((4096, 128), F32), i...  2.37 us

profile of v5, /device:TPU:1, one launch (start us, length us, event | category | flops | bytes accessed | tf_op | source)
XLA Modules:
  0.0 67.5 jit_solution(14489605114201813934)
XLA Ops:
  0.0 65.1 %shard_map.82 = bf16[2,8,256,128]{3,2,1,0:T(8,128)(2,1)} custom-call(bf16[1024,1024]{1,0:T(8,128)(2,1)} %bitcast.5, bf16[1024,1024]{1,0:T(8,128)(2,1)} %bitcast.6, bf16[1024,128]{1,0:T(8,128)(2,1)} %pin.1, bf16[1024,128]{1,0:T(8,128)(2,1)} %pout.1, f32[2048,1024]{1,0:T(8,128)} %fish.1, bf16[4096,1024]{1,0:T(8,128)(2,1)} %store.1, s32[16]{0:T(128)} %lens_in.1, ...), custom_call_target="tpu_custom_call" | custom-call | tf_op jit(solution)/shard_map/pallas_call | solution.py:452
  65.2 2.4 %shard_map.83 = f32[4096,128]{1,0:T(8,128)} custom-call(bf16[4096,128]{1,0:T(8,128)(2,1)} %bitcast.4), custom_call_target="tpu_custom_call" | custom-call | tf_op jit(solution)/shard_map/pallas_call | solution.py:474
